TPU v7x, 256 devices: a whole 4x4x8 slice. The times are simulated.
256 devices in a mesh: occ: 64 (over x, y_lo, z), pair: 4 (over y_hi, core).
Axes of the slice: x: 4, y: 4 (y_hi: 2, y_lo: 2; y = y_hi * 2 + y_lo), z: 8, core: 2. Of those that a mesh axis runs over, the one named last changes fastest.
Arguments:
- three_index: float32 [256, 256, 5120], P(('occ', 'pair')), may hold values from -0.72 to 0.72
- occ_energy: float32 [256], replicated, may hold values from -2 to -0.5
- vir_energy: float32 [256], replicated, may hold values from 0.5 to 4
- coeff: float32 [256, 256], replicated, may hold values from -0.375 to 0.375
- kept: int32 [256, 24], P(('occ', 'pair')), may hold values from 0 to 39, as said below
- owner_slot: int32 [40], replicated, may hold values from 0 to 63, as said below
Outputs:
- pair_energy: float32 [256, 4], P(('occ', 'pair'))
- back_density: bfloat16 [64, 256, 256, 128], P('occ', None, 'pair')
Inputs may be any that keep to these rules, and one draw needn't show every extreme that they name: Each row names 24 different blocks; some blocks are kept by far more orbitals than others. `owner_slot`: different blocks have different slots; slot s belongs to owner s.
All inputs are finite; a program needn't handle non-finite values.
Results may differ from a plain program's by a relative error of at most 0.001.
Values sent between devices are 32-bit elements; how exact they have to be, the bound alone decides.
A program may use at most 128 MiB of HBM per device.

v0:
```python
import jax
import jax.numpy as jnp
from jax import lax
from jax.sharding import PartitionSpec as P

BLOCK = 128


def partner_terms(own_rows, own_energy, partner_rows, partner_energy, vir_energy):
    integrals = jnp.einsum("ap,jbp->jab", own_rows, partner_rows, precision=lax.Precision.HIGHEST)
    denominator = (
        own_energy
        + partner_energy[:, None, None]
        - vir_energy[None, :, None]
        - vir_energy[None, None, :]
    )
    scaled = (2.0 * integrals - jnp.swapaxes(integrals, 1, 2)) / denominator
    energies = jnp.sum(integrals * scaled, axis=(1, 2))
    density = jnp.einsum("jab,jbp->ap", scaled, partner_rows, precision=lax.Precision.HIGHEST)
    return (density, energies)


def shards(three_index, occ_energy, vir_energy, coeff, kept, owner_slot):
    pair_count = lax.axis_size("pair")
    occ_count = lax.axis_size("occ")
    group_first = lax.axis_index("occ") * pair_count
    my_place = lax.axis_index("pair")
    group_energy = lax.dynamic_slice_in_dim(occ_energy, group_first, pair_count)
    own_energy = lax.dynamic_slice_in_dim(group_energy, my_place, 1)[0]
    vir_count = three_index.shape[1]
    aux_count = three_index.shape[2]
    own_rows = three_index[0]
    partner_rows = lax.all_gather(three_index, "pair", axis=0, tiled=True)
    partner_count = partner_rows.shape[0]
    density, energies = partner_terms(own_rows, own_energy, partner_rows, group_energy, vir_energy)
    places = jnp.arange(partner_count, dtype=jnp.int32)
    onehot = (places[:, None] == jnp.arange(pair_count, dtype=jnp.int32)[None, :]).astype(
        jnp.float32
    )
    energy_row = jnp.dot(energies, onehot, precision=lax.Precision.HIGHEST)
    pair_energy = energy_row[None, :]
    block_count = aux_count // BLOCK
    own_max = -(-block_count // occ_count)
    slot_total = own_max * occ_count
    block_ids = jnp.arange(block_count, dtype=jnp.int32)
    slot_ids = jnp.arange(slot_total, dtype=jnp.int32)
    matches = (owner_slot[None, :] == slot_ids[:, None]).astype(jnp.int32)
    block_of_slot = jnp.sum(matches * block_ids[None, :], axis=1)
    slot_used = jnp.sum(matches, axis=1) > 0
    kept_blocks = jnp.any(kept[0][:, None] == block_ids[None, :], axis=0)
    slot_live = jnp.logical_and(slot_used, kept_blocks[block_of_slot])
    block_major = density.reshape(vir_count, block_count, BLOCK).transpose(1, 0, 2)
    slot_order = block_of_slot.reshape(occ_count, own_max).T
    live_order = slot_live.reshape(occ_count, own_max).T.astype(jnp.float32)
    outgoing = jnp.take(block_major, slot_order, axis=0) * live_order[:, :, None, None]
    outgoing = outgoing[:, :, None]
    quarters = lax.all_to_all(outgoing, "pair", split_axis=3, concat_axis=2, tiled=True)
    received = lax.all_to_all(quarters, "occ", split_axis=1, concat_axis=1, tiled=True)
    item_count = received.shape[0]
    flattened = received.reshape(item_count, coeff.shape[1], -1)
    result = jnp.einsum("mi,sic->smc", coeff, flattened, precision=lax.Precision.HIGHEST)
    back_density = result.reshape(item_count, coeff.shape[0], -1, BLOCK).astype(jnp.bfloat16)
    return (pair_energy, back_density)


def solution(mesh):
    in_specs = (P(("occ", "pair"), None, None), P(), P(), P(), P(("occ", "pair"), None), P())
    out_specs = (P(("occ", "pair"), None), P("occ", None, "pair", None))
    return jax.shard_map(shards, mesh=mesh, in_specs=in_specs, out_specs=out_specs, check_vma=False)
```

profile of v0, /device:TPU:42, one launch (start us, length us, event | category | flops | bytes accessed | tf_op | source)
XLA Modules:
  0.0 547.7 jit_solution(13521295028976477015)
XLA Ops:
  7.2 0.0 copy-start
  7.2 0.0 all-gather.2.cloned.1.call-start
  7.2 0.7 all-gather.2.cloned.1.call-update
  7.9 1.3 dynamic_slice.9
  9.2 0.7 convert_reduce_fusion
  10.0 0.7 fusion.9
  10.7 0.8 gather_fusion.1
  11.5 1.4 dynamic-slice_add_fusion
  12.9 0.8 broadcast_subtract_fusion
  13.7 0.0 copy-start.1
  13.7 136.0 %all-gather.2.cloned.1.call-done = f32[4,256,5120]{2,1,0:T(8,128)} async-done(((f32[1,256,5120]{2,1,0:T(8,128)}), f32[4,256,5120]{2,1,0:T(8,128)}) %all-gather.2.cloned.1.call-update) | async-done | bytes 20971536 | tf_op jit(solution)/shard_map/all_gather | solution.py:33
  149.6 20.0 %fusion.3 = f32[4,256,256]{2,1,0:T(8,128)S(1)} fusion(f32[4,256,5120]{2,1,0:T(8,128)} %all-gather.2.cloned.1.call-done, f32[1,256,5120]{2,1,0:T(8,128)} %param.6), kind=kOutput, calls=%fused_computation.8 | convolution fusion | flops 16106127360 | bytes 27262976 | tf_op jit(solution)/shard_map/ap,jbp->jab/dot_general | solution.py:10
  169.6 0.3 copy.18
  169.9 0.0 copy-done.1
  170.0 21.4 %convolution_bitcast_fusion = f32[32,40,8,128]{3,2,1,0:T(8,128)S(1)} fusion(f32[4,256,5120]{2,1,0:T(8,128)} %all-gather.2.cloned.1.call-done, f32[4,256,256]{2,1,0:T(8,128)S(1)} %fusion.3, f32[4,256,256]{1,2,0:T(8,128)S(1)} %copy.18, f32[256]{0:T(256)S(1)} %copy-done.1, f32[4,256]{1,0:T(4,128)S(1)} %broadcast_subtract_fusion), kind=kOutput, calls=%fused_computation.10 | convolution fusion | flops 16107175936 | bytes 28316672 | tf_op jit(solution)/shard_map/jab,jbp->ap/dot_general | solution.py:19
  191.3 3.1 copy.30
  194.4 6.8 %gather_fusion = f32[64,256,128]{2,1,0:T(8,128)} fusion(f32[40,256,128]{2,1,0:T(8,128)} %bitcast.58, s32[1024]{0:T(1024)S(1)} %pad_clamp_fusion.1), kind=kCustom, calls=%fused_computation | custom fusion | bytes 16777472 | tf_op jit(solution)/shard_map/jit(_take)/gather | solution.py:55
  201.2 4.9 fusion.2
  206.0 4.9 copy.20
  210.9 97.3 %all_to_all.17 = f32[1,64,1,256,128]{4,1,2,0,3:T(8,128)S(1)} all-to-all(f32[1,64,1,256,128]{4,1,2,0,3:T(8,128)S(1)} %copy.20), channel_id=1, replica_groups=mesh['occ'=64,'pair'=4] {'pair'}, dimensions={3} | all-to-all | bytes 16777216 | tf_op jit(solution)/shard_map/all_to_all | solution.py:57
  308.2 8.1 %copy.21 = f32[1,64,4,64,128]{4,3,2,0,1:T(8,128)} copy(f32[1,64,4,64,128]{4,1,3,2,0:T(8,128)S(1)} %bitcast.59) | data formatting | bytes 16777216 | tf_op jit(solution)/shard_map/all_to_all | solution.py:57
  316.3 11.6 %all-to-all-start.1 = ((f32[1,64,4,64,128]{4,3,2,0,1:T(8,128)}), f32[1,64,4,64,128]{4,3,2,0,1:T(8,128)}, u32[]{:S(2)}, u32[]{:S(2)}) async-start(f32[1,64,4,64,128]{4,3,2,0,1:T(8,128)} %copy.21), calls=%async_computation.1 | async-start | bytes 16777216 | tf_op jit(solution)/shard_map/all_to_all | solution.py:58
  327.9 0.4 fusion.7
  328.3 0.6 fusion.10
  328.9 184.2 %all-to-all-done.1 = f32[1,64,4,64,128]{4,3,2,0,1:T(8,128)} async-done(((f32[1,64,4,64,128]{4,3,2,0,1:T(8,128)}), f32[1,64,4,64,128]{4,3,2,0,1:T(8,128)}, u32[]{:S(2)}, u32[]{:S(2)}) %all-to-all-start.1) | async-done | bytes 8388640 | tf_op jit(solution)/shard_map/all_to_all | solution.py:58
  513.1 0.0 copy-done
  513.1 21.3 %convolution_convert_fusion = bf16[8192,256]{1,0:T(8,128)(2,1)} fusion(f32[256,256]{1,0:T(8,128)S(1)} %copy-done, f32[32,8,64,128]{3,2,1,0:T(8,128)} %bitcast.24), kind=kOutput, calls=%fused_computation.2 | convolution fusion | flops 6444548096 | bytes 12845056 | tf_op jit(solution)/shard_map/mi,sic->smc/dot_general | solution.py:61
  534.4 6.4 %copy.22 = bf16[1,256,64,128]{3,2,1,0:T(8,128)(2,1)} copy(bf16[1,256,64,128]{1,3,2,0:T(8,128)(2,1)} %bitcast.60) | data formatting | bytes 8388608
  (5 shorter events, 0.0 us)
Async XLA Ops:
  7.2 505.9 %copy-start = (f32[256,256]{1,0:T(8,128)S(1)}, f32[256,256]{1,0:T(8,128)}, u32[]{:S(2)}) copy-start(f32[256,256]{1,0:T(8,128)} %param.9) | copy-start | bytes 786436
  7.2 142.5 %all-gather.2.cloned.1.call-start = ((), (), s32[]{:S(2)}) async-start(), calls=%async_computation.2 | async-start | bytes 26214400 | tf_op jit(solution)/shard_map/all_gather | solution.py:33
  13.7 156.3 %copy-start.1 = (f32[256]{0:T(256)S(1)}, f32[256]{0:T(256)}, u32[]{:S(2)}) copy-start(f32[256]{0:T(256)} %param.8) | copy-start | bytes 3076
  316.3 196.8 %all-to-all-start.1 = ((f32[1,64,4,64,128]{4,3,2,0,1:T(8,128)}), f32[1,64,4,64,128]{4,3,2,0,1:T(8,128)}, u32[]{:S(2)}, u32[]{:S(2)}) async-start(f32[1,64,4,64,128]{4,3,2,0,1:T(8,128)} %copy.21), calls=%async_computation.1 | async-start | bytes 16777216 | tf_op jit(solution)/shard_map/all_to_all | solution.py:58
Sparse Core Ops, SparseCore 0:
  9.8 139.7 all-gather.1
where the time goes:
time: 548 us
  waiting for transfers between devices  321 us (59%)
  blocking collectives  97.3 us (18%)
  matrix products  63.3 us (12%)
  local copies, waits for them, and re-layouts  31.6 us (6%)
  between operations  14.1 us (3%)
  starting transfers between devices  11.6 us (2%)
  other arithmetic  8.94 us (2%)
    all_to_all x1, waiting for transfers between devices, shards(): lax.all_to_all(quarters, 'occ', split_axis=1, concat_axis=1, tiled=True)  184 us
    all_gather x1, waiting for transfers between devices, shards(): partner_rows = lax.all_gather(three_index, 'pair', axis=0, tiled=True)  136 us
    all_to_all x1, blocking collectives, shards(): lax.all_to_all(outgoing, 'pair', split_axis=3, concat_axis=2, tiled=True)  97.3 us
    dot_general x1, matrix products, partner_terms(): jnp.einsum('jab,jbp->ap', scaled, partner_rows, precision=lax.Precision.H...  21.4 us
    dot_general x1, matrix products, shards(): jnp.einsum('mi,sic->smc', coeff, flattened, precision=lax.Precision.HIGHEST)  21.3 us
    dot_general x1, matrix products, partner_terms(): jnp.einsum('ap,jbp->jab', own_rows, partner_rows, precision=lax.Precision...  20 us
    all_to_all x1, starting transfers between devices, shards(): lax.all_to_all(quarters, 'occ', split_axis=1, concat_axis=1, tiled=True)  11.6 us
  transfers between devices with their start and end apart: 2, of which 2 were waited for; matrix products, arithmetic and copies ran while one was open for 1% of the time, Pallas kernels for 0%

commit v1 on v0

v1 whole, which is shorter than its diff:
```python
import jax
import jax.numpy as jnp
from jax import lax
from jax.sharding import PartitionSpec as P

BLOCK = 128
PREC = lax.Precision.HIGH


def shards(three_index, occ_energy, vir_energy, coeff, kept, owner_slot):
    pair_count = lax.axis_size("pair")
    occ_count = lax.axis_size("occ")
    group_first = lax.axis_index("occ") * pair_count
    my_place = lax.axis_index("pair")
    group_energy = lax.dynamic_slice_in_dim(occ_energy, group_first, pair_count)
    vir_count = three_index.shape[1]
    aux_count = three_index.shape[2]
    quarter = vir_count // pair_count
    block_count = aux_count // BLOCK
    block_ids = jnp.arange(block_count, dtype=jnp.int32)
    kept_own = jnp.any(kept[0][:, None] == block_ids[None, :], axis=0).astype(jnp.float32)
    live = lax.all_gather(kept_own[None], "pair", axis=0, tiled=True)
    rows = lax.all_gather(three_index, "pair", axis=0, tiled=True)
    mine = lax.dynamic_slice_in_dim(rows, my_place * quarter, quarter, axis=1)
    integrals = jnp.einsum("iap,jbp->iajb", mine, rows, precision=PREC)
    my_vir = lax.dynamic_slice_in_dim(vir_energy, my_place * quarter, quarter)
    denominator = (
        group_energy[:, None, None, None]
        + group_energy[None, None, :, None]
        - my_vir[None, :, None, None]
        - vir_energy[None, None, None, :]
    )
    scaled = (2.0 * integrals - jnp.transpose(integrals, (2, 1, 0, 3))) / denominator
    energies = lax.psum(jnp.sum(integrals * scaled, axis=(1, 3)), "pair")
    pair_energy = lax.dynamic_slice_in_dim(energies, my_place, 1, axis=0)
    density = jnp.einsum("iajb,jbp->iap", scaled, rows, precision=PREC)

    slot_ids = jnp.arange(occ_count, dtype=jnp.int32)
    matches = (owner_slot[None, :] == slot_ids[:, None]).astype(jnp.int32)
    block_of_slot = jnp.sum(matches * block_ids[None, :], axis=1)
    slot_used = jnp.sum(matches, axis=1) > 0
    slot_live = jnp.take(live, block_of_slot, axis=1).T * slot_used[:, None].astype(jnp.float32)
    block_major = density.reshape(pair_count, quarter, block_count, BLOCK).transpose(2, 0, 1, 3)
    outgoing = jnp.take(block_major, block_of_slot, axis=0) * slot_live[:, :, None, None]
    received = lax.all_to_all(outgoing, "occ", split_axis=0, concat_axis=0, tiled=True)
    flattened = received.reshape(coeff.shape[1], quarter, BLOCK)
    result = jnp.einsum("mi,iap->map", coeff, flattened, precision=PREC)
    return (pair_energy, result[None].astype(jnp.bfloat16))


def solution(mesh):
    in_specs = (P(("occ", "pair"), None, None), P(), P(), P(), P(("occ", "pair"), None), P())
    out_specs = (P(("occ", "pair"), None), P("occ", None, "pair", None))
    return jax.shard_map(shards, mesh=mesh, in_specs=in_specs, out_specs=out_specs, check_vma=False)
```

time: 548 us -> 427 us (0.78)
  blocking collectives: 97.3 us -> 8.41 us
  matrix products: 63.3 us -> 42 us
  local copies, waits for them, and re-layouts: 31.6 us -> 20.4 us
    all_to_all x1 -> x0, blocking collectives: 97.3 us -> none  [shards(): lax.all_to_all(outgoing, 'pair', split_axis=3, concat_axis=2, tiled=True)]
    dot_general x4 -> x3, matrix products: 63.3 us -> 42 us  [the longest x1 15.2 us: shards(): result = jnp.einsum('mi,iap->map', coeff, flattened, precision=PREC)]
    psum x0 -> x1, blocking collectives: none -> 8.41 us  [shards(): energies = lax.psum(jnp.sum(integrals * scaled, axis=(1, 3)), 'pair')]
    all_to_all x1 -> x0, local copies, waits for them, and re-layouts: 8.06 us -> none  [shards(): lax.all_to_all(outgoing, 'pair', split_axis=3, concat_axis=2, tiled=True)]
where the time goes in v1:
time: 427 us; the launch traced here: 426 us
  waiting for transfers between devices  321 us (75%)
  matrix products  42 us (10%)
  local copies, waits for them, and re-layouts  20.4 us (5%)
  between operations  14.8 us (3%)
  starting transfers between devices  11.6 us (3%)
  blocking collectives  8.41 us (2%)
  other arithmetic  8.15 us (2%)
    all_to_all x1, waiting for transfers between devices, shards(): lax.all_to_all(outgoing, 'occ', split_axis=0, concat_axis=0, tiled=True)  184 us
    all_gather x1, waiting for transfers between devices, shards(): rows = lax.all_gather(three_index, 'pair', axis=0, tiled=True)  137 us
    dot_general x1, matrix products, shards(): result = jnp.einsum('mi,iap->map', coeff, flattened, precision=PREC)  15.2 us
    dot_general x1, matrix products, shards(): integrals = jnp.einsum('iap,jbp->iajb', mine, rows, precision=PREC)  13.7 us
    dot_general x1, matrix products, shards(): density = jnp.einsum('iajb,jbp->iap', scaled, rows, precision=PREC)  13 us
    all_to_all x1, starting transfers between devices, shards(): lax.all_to_all(outgoing, 'occ', split_axis=0, concat_axis=0, tiled=True)  11.6 us
  transfers between devices with their start and end apart: 2, of which 2 were waited for; matrix products, arithmetic and copies ran while one was open for 1% of the time, Pallas kernels for 0%

profile of v1, /device:TPU:42, one launch (start us, length us, event | category | flops | bytes accessed | tf_op | source)
XLA Modules:
  0.0 426.3 jit_solution(14839481976655269999)
XLA Ops:
  7.2 0.0 copy-start
  7.2 0.0 all-gather.3.cloned.1.call-start
  7.2 0.7 all-gather.3.cloned.1.call-update
  7.9 0.8 dynamic_slice.14
  8.7 0.8 dynamic_slice.13
  9.4 1.3 dynamic-slice
  11.3 0.7 convert_reduce_fusion
  12.1 0.7 fusion.19
  12.9 0.1 convert_dynamic-update-slice_fusion
  13.0 0.1 broadcast_add_fusion
  13.1 0.1 broadcast_subtract_fusion
  13.1 0.0 copy-start.1
  13.1 136.5 %all-gather.3.cloned.1.call-done = f32[4,256,5120]{2,1,0:T(8,128)} async-done(((f32[1,256,5120]{2,1,0:T(8,128)}), f32[4,256,5120]{2,1,0:T(8,128)}) %all-gather.3.cloned.1.call-update) | async-done | bytes 20971536 | tf_op jit(solution)/shard_map/all_gather | solution.py:23
  149.6 13.7 %fusion.2 = f32[4,64,4,256]{3,1,2,0:T(8,128)S(1)} fusion(f32[4,256,5120]{2,1,0:T(8,128)} %all-gather.3.cloned.1.call-done, s32[]{:T(128)S(6)} %select_n.38), kind=kOutput, calls=%fused_computation.4 | convolution fusion | flops 8053063680 | bytes 27262980 | tf_op jit(solution)/shard_map/iap,jbp->iajb/dot_general | solution.py:25
  163.4 0.0 copy-done.1
  163.4 0.4 multiply_reduce_fusion
  163.8 13.0 %fusion.10 = f32[4,8,40,8,128]{4,3,2,1,0:T(8,128)S(1)} fusion(f32[4,256,5120]{2,1,0:T(8,128)} %all-gather.3.cloned.1.call-done, f32[4,64,4,256]{3,1,2,0:T(8,128)S(1)} %fusion.2, f32[256]{0:T(256)S(1)} %copy-done.1, f32[4,64,4]{1,2,0:T(4,128)S(1)} %broadcast_subtract_fusion), kind=kOutput, calls=%fused_computation.13 | convolution fusion | flops 8054112256 | bytes 27268096 | tf_op jit(solution)/shard_map/iajb,jbp->iap/dot_general | solution.py:36
  176.8 3.0 copy.39
  179.9 8.4 %all-reduce.1 = (f32[4,4]{1,0:T(4,128)S(1)}, f32[160]{0:T(256)S(1)}) all-reduce(f32[4,4]{1,0:T(4,128)S(1)} %multiply_reduce_fusion, f32[160]{0:T(256)S(1)} %convert_dynamic-update-slice_fusion), channel_id=1, replica_groups=mesh['occ'=64,'pair'=4] {'pair'}, use_global_device_ids=true, to_apply=%region_1.0 | all-reduce | flops 176 | bytes 1408 | tf_op jit(solution)/shard_map/psum | solution.py:34
  188.3 0.1 reshape.104
  188.4 0.1 copy.24
  188.5 6.8 %gather_fusion = f32[64,4,64,128]{3,2,1,0:T(8,128)} fusion(f32[40,4,64,128]{3,2,1,0:T(8,128)} %bitcast.43, s32[1024]{0:T(1024)S(1)} %pad_clamp_fusion), kind=kCustom, calls=%fused_computation | custom fusion | bytes 16777472 | tf_op jit(solution)/shard_map/jit(_take)/gather | solution.py:44
  195.3 0.6 gather_fusion.1
  195.8 0.1 select_multiply_fusion.1
  195.9 5.9 %select_multiply_fusion = f32[64,4,64,128]{3,2,1,0:T(8,128)} fusion(f32[64,4,64,128]{3,2,1,0:T(8,128)} %gather_fusion, f32[64,4]{1,0:T(8,128)S(1)} %select_multiply_fusion.1, pred[64]{0:T(512)(128)(4,1)S(1)} %compare_and_fusion), kind=kLoop, calls=%fused_computation.8 | loop fusion | flops 4194304 | bytes 16778304 | tf_op jit(solution)/shard_map/mul | solution.py:44
  201.8 11.6 %all-to-all-start = ((f32[64,4,64,128]{3,2,1,0:T(8,128)}), f32[64,4,64,128]{3,2,1,0:T(8,128)}, u32[]{:S(2)}, u32[]{:S(2)}) async-start(f32[64,4,64,128]{3,2,1,0:T(8,128)} %select_multiply_fusion), calls=%async_computation | async-start | bytes 16777216 | tf_op jit(solution)/shard_map/all_to_all | solution.py:45
  213.4 0.5 constant_dynamic-slice_fusion
  214.0 183.8 %all-to-all-done = f32[64,4,64,128]{3,2,1,0:T(8,128)} async-done(((f32[64,4,64,128]{3,2,1,0:T(8,128)}), f32[64,4,64,128]{3,2,1,0:T(8,128)}, u32[]{:S(2)}, u32[]{:S(2)}) %all-to-all-start) | async-done | bytes 8388640 | tf_op jit(solution)/shard_map/all_to_all | solution.py:45
  397.7 0.0 copy-done
  397.7 15.2 %convert_bitcast_fusion = bf16[1,256,64,128]{1,3,2,0:T(8,128)(2,1)} fusion(f32[256,64,128]{2,1,0:T(8,128)} %bitcast.11, f32[256,256]{1,0:T(8,128)S(1)} %copy-done), kind=kOutput, calls=%fused_computation.12 | convolution fusion | flops 3223322624 | bytes 12845056 | tf_op jit(solution)/shard_map/mi,iap->map/dot_general | solution.py:47
  413.0 6.4 %copy.26 = bf16[1,256,64,128]{3,2,1,0:T(8,128)(2,1)} copy(bf16[1,256,64,128]{1,3,2,0:T(8,128)(2,1)} %convert_bitcast_fusion) | data formatting | bytes 8388608
  (5 shorter events, 0.0 us)
Async XLA Ops:
  7.2 390.6 %copy-start = (f32[256,256]{1,0:T(8,128)S(1)}, f32[256,256]{1,0:T(8,128)}, u32[]{:S(2)}) copy-start(f32[256,256]{1,0:T(8,128)} %param.9) | copy-start | bytes 786436
  7.2 142.5 %all-gather.3.cloned.1.call-start = ((), (), s32[]{:S(2)}) async-start(), calls=%async_computation.1 | async-start | bytes 26214400 | tf_op jit(solution)/shard_map/all_gather | solution.py:23
  13.1 150.2 %copy-start.1 = (f32[256]{0:T(256)S(1)}, f32[256]{0:T(256)}, u32[]{:S(2)}) copy-start(f32[256]{0:T(256)} %param.8) | copy-start | bytes 3076
  201.8 195.9 %all-to-all-start = ((f32[64,4,64,128]{3,2,1,0:T(8,128)}), f32[64,4,64,128]{3,2,1,0:T(8,128)}, u32[]{:S(2)}, u32[]{:S(2)}) async-start(f32[64,4,64,128]{3,2,1,0:T(8,128)} %select_multiply_fusion), calls=%async_computation | async-start | bytes 16777216 | tf_op jit(solution)/shard_map/all_to_all | solution.py:45
Sparse Core Ops, SparseCore 0:
  9.8 139.7 all-gather.2
